TPU v7x, 32 devices: a whole 2x2x4 slice. The times are simulated.
32 devices in a mesh: dp: 4 (over y, core), cells: 8 (over z, x).
Axes of the slice: x: 2, y: 2, z: 4, core: 2. Of those that a mesh axis runs over, the one named last changes fastest.
Arguments:
- jac_blocks: bfloat16 [32, 128, 8192], P('dp', None, 'cells'), may hold values from -6 to 6
- slot_cell_blocks: int32 [32, 64], P('dp', 'cells'), may hold values from 0 to 15, as said below
- live_counts: int32 [32, 8], P('dp', 'cells'), may hold values from 1 to 8, as said below
- eigen_basis: bfloat16 [16384, 1536], P('cells', 'dp'), may hold values from -0.0625 to 0.0625
- weights: float32 [4096], P(('dp', 'cells')), may hold values from 0.25 to 4
- residual: float32 [4096], P(('dp', 'cells')), may hold values from -6 to 6
Outputs:
- jq: float32 [4096, 1536], P(('dp', 'cells'))
- system: float32 [1536, 1536], P('cells')
- rhs: float32 [1536], P('cells')
Inputs may be any that keep to these rules, and one draw needn't show every extreme that they name: `slot_cell_blocks`: within one data block and one slab, the 8 entries name distinct cell blocks; only the first live_counts entries are used. `live_counts`: every data block has 8 live slots in some slab.
All inputs are finite; a program needn't handle non-finite values.
Results may differ from a plain program's by a relative error of at most 0.0003.
Values may be sent and summed in bfloat16 or wider, within the bound.
A program may use at most 128 MiB of HBM per device.

v0:
```python
import math

import jax
import jax.numpy as jnp
from jax import lax
from jax.sharding import PartitionSpec as P


def on_device(jac_blocks, slot_cell_blocks, live_counts, eigen_basis, weights, residual):
    basis = lax.all_gather(eigen_basis, "dp", axis=1, tiled=True)
    block_width = basis.shape[1]
    block_tile = jac_blocks.shape[1]
    slot_count = slot_cell_blocks.shape[1]
    stacked_blocks = basis.reshape(basis.shape[0] // block_tile, block_tile, block_width)
    n_cells = lax.axis_size("cells")
    n_groups = lax.axis_size("dp")
    ndata = weights.shape[0] * n_cells * n_groups

    def block_term(jacobian_row, column_range, active_slot):
        retain_flag = (lax.iota(jnp.int32, slot_count) < active_slot).astype(jnp.bfloat16)
        masked_entries = (
            jacobian_row.reshape(block_tile, slot_count, block_tile) * retain_flag[None, :, None]
        ).reshape(block_tile, slot_count * block_tile)
        selected_rows = stacked_blocks[column_range].reshape(slot_count * block_tile, block_width)
        return jnp.dot(masked_entries, selected_rows, preferred_element_type=jnp.float32)

    own_rows = jac_blocks.shape[0] * block_tile // n_cells
    terms = lax.map(
        lambda items: block_term(items[0], items[1], items[2]),
        (jac_blocks, slot_cell_blocks, live_counts[:, 0]),
    )
    jq = lax.psum_scatter(
        terms.reshape(lax.axis_size("cells") * own_rows, block_width),
        "cells",
        scatter_dimension=0,
        tiled=True,
    )
    weighted = jq * weights[:, None]
    gram_term = (
        lax.dot_general(jq, weighted, (((0,), (0,)), ((), ())), precision=lax.Precision.HIGHEST)
        / ndata
    )
    rhs_term = lax.dot_general(
        jq, weights * residual, (((0,), (0,)), ((), ())), precision=lax.Precision.HIGHEST
    ) / math.sqrt(ndata)
    gram_part, rhs_part = (
        lax.psum_scatter(gram_term, "cells", scatter_dimension=0, tiled=True),
        lax.psum_scatter(rhs_term, "cells", scatter_dimension=0, tiled=True),
    )
    gram_sum, rhs_sum = lax.psum((gram_part, rhs_part), "dp")
    rows_here = block_width // n_cells
    row_ids = lax.axis_index("cells") * rows_here + lax.iota(jnp.int32, rows_here)
    identity = (row_ids[:, None] == lax.iota(jnp.int32, block_width)[None, :]).astype(jnp.float32)
    system = gram_sum + identity
    return (jq, system, rhs_sum)


def solution(mesh):
    placed = (
        P("dp", None, "cells"),
        P("dp", "cells"),
        P("dp", "cells"),
        P("cells", "dp"),
        P(("dp", "cells")),
        P(("dp", "cells")),
    )
    return jax.shard_map(
        on_device,
        mesh=mesh,
        in_specs=placed,
        out_specs=(P(("dp", "cells"), None), P("cells", None), P("cells")),
        check_vma=False,
    )
```

profile of v0, /device:TPU:1, one launch (start us, length us, event | category | flops | bytes accessed | tf_op | source)
XLA Modules:
  0.0 476.9 jit_solution(17630316756467067911)
XLA Ops:
  8.0 50.4 %all-gather.2.cloned.1.call-done = bf16[2048,1536]{1,0:T(8,128)(2,1)} async-done(((bf16[2048,384]{1,0:T(8,128)(2,1)}), bf16[2048,1536]{1,0:T(8,128)(2,1)}) %all-gather.2.cloned.1.call-update) | async-done | bytes 6291472 | tf_op jit(solution)/shard_map/all_gather | solution.py:10
  58.4 79.2 %while.10 = (s32[]{:T(128)}, f32[8,128,1536]{2,1,0:T(8,128)}, bf16[8,128,1024]{2,1,0:T(8,128)(2,1)}, s32[8]{0:T(128)}, s32[8,8]{1,0:T(8,128)}, /*index=5*/bf16[16,128,1536]{2,1,0:T(8,128)(2,1)}, s32[]{:T(128)}) while((s32[]{:T(128)}, f32[8,128,1536]{2,1,0:T(8,128)}, bf16[8,128,1024]{2,1,0:T(8,128)(2,1)}, s32[8]{0:T(128)}, s32[8,8]{1,0:T(8,128)}, ...), condition=%wide.region_1.2_spmd, body=%wide.region_0.1_spmd.sunk | while | flops 402785312 | bytes 11539361 | solution.py:28
  58.4 0.7 fusion.18
  59.1 3.5 gather_fusion
  62.6 1.7 constant_dynamic-slice_fusion.3
  64.3 1.1 copy.16
  66.7 1.6 fusion.19
  68.3 0.7 fusion.18
  69.0 3.5 gather_fusion
  72.5 1.7 constant_dynamic-slice_fusion.3
  74.2 1.1 copy.16
  76.6 1.6 fusion.19
  78.1 0.7 fusion.18
  78.8 3.5 gather_fusion
  82.4 1.7 constant_dynamic-slice_fusion.3
  84.1 1.1 copy.16
  86.4 1.6 fusion.19
  88.1 0.7 fusion.18
  88.8 3.5 gather_fusion
  92.3 1.7 constant_dynamic-slice_fusion.3
  94.0 1.1 copy.16
  96.4 1.6 fusion.19
  98.0 0.7 fusion.18
  98.8 3.5 gather_fusion
  102.3 1.7 constant_dynamic-slice_fusion.3
  104.0 1.1 copy.16
  106.4 1.6 fusion.19
  107.9 0.7 fusion.18
  108.7 3.5 gather_fusion
  112.2 1.7 constant_dynamic-slice_fusion.3
  113.9 1.1 copy.16
  116.3 1.6 fusion.19
  117.9 0.7 fusion.18
  118.6 3.5 gather_fusion
  122.1 1.7 constant_dynamic-slice_fusion.3
  123.8 1.1 copy.16
  126.2 1.6 fusion.19
  128.5 3.5 gather_fusion
  132.0 1.7 constant_dynamic-slice_fusion.3
  133.7 1.1 copy.16
  136.1 1.6 fusion.19
  137.7 116.8 %reduce-scatter.3.cloned.1.call-done = f32[128,1536]{1,0:T(8,128)} async-done(((f32[1024,1536]{1,0:T(8,128)}), f32[128,1536]{1,0:T(8,128)}) %reduce-scatter.3.cloned.1.call-update) | async-done | bytes 786448 | tf_op jit(solution)/shard_map/reduce_scatter | solution.py:32
  254.6 11.3 %convolution_multiply_fusion = f32[1536,1536]{1,0:T(8,128)} fusion(f32[128,1536]{1,0:T(8,128)} %reduce-scatter.3.cloned.1.call-done, f32[128]{0:T(128)S(1)} %copy-done.1), kind=kOutput, calls=%fused_computation.12 | convolution fusion | flops 3626434560 | bytes 10224128 | tf_op jit(solution)/shard_map/dot_general | solution.py:40
  265.9 163.4 %reduce-scatter.5.cloned.1.call-done = f32[192,1536]{1,0:T(8,128)} async-done(((f32[1536,1536]{1,0:T(8,128)}), f32[192,1536]{1,0:T(8,128)}) %reduce-scatter.5.cloned.1.call-update) | async-done | bytes 1179664 | tf_op jit(solution)/shard_map/reduce_scatter | solution.py:47
  431.2 16.1 %all-reduce = f32[1536]{0:T(1024)S(1)} all-reduce(f32[1536]{0:T(1024)S(1)} %broadcast_multiply_fusion), channel_id=4, replica_groups=mesh['dp'=4,'cells'=8] {'cells'}, use_global_device_ids=true, to_apply=%region_5.6.clone | all-reduce | flops 1536 | bytes 12288
  447.4 9.7 %psum.15 = f32[192]{0:T(256)} all-reduce(f32[192]{0:T(256)S(1)} %dynamic-slice.1), channel_id=1, replica_groups=mesh['dp'=4,'cells'=8] {'dp'}, use_global_device_ids=true, to_apply=%region_6.7 | all-reduce | flops 192 | bytes 1536 | tf_op jit(solution)/shard_map/psum | solution.py:50
  457.1 10.8 %all-reduce.3.cloned.1.call-done = f32[192,1536]{1,0:T(8,128)} async-done(((f32[192,1536]{1,0:T(8,128)}), f32[192,1536]{1,0:T(8,128)}) %all-reduce.3.cloned.1.call-update) | async-done | bytes 1179664 | tf_op jit(solution)/shard_map/psum | solution.py:50
  467.9 2.5 convert_add_fusion
  (63 shorter events, 12.8 us)
Async XLA Ops:
  7.2 51.2 %all-gather.2.cloned.1.call-start = ((), (), s32[]{:S(2)}) async-start(), calls=%async_computation.2 | async-start | bytes 7864320 | tf_op jit(solution)/shard_map/all_gather | solution.py:10
  7.9 246.7 %reduce-scatter.3.cloned.1.call-start = ((), (), s32[]{:S(2)}) async-start(), calls=%async_computation.3 | async-start | bytes 7077888 | tf_op jit(solution)/shard_map/reduce_scatter | solution.py:32
  59.1 6.4 %copy-start.3 = (s32[8]{0:T(128)S(1)}, s32[8]{0:T(128)}, u32[]{:S(2)}) copy-start(s32[8]{0:T(128)} %get-tuple-element.114) | copy-start | bytes 100 | tf_op jit(solution)/shard_map/while
  69.0 6.4 %copy-start.3 = (s32[8]{0:T(128)S(1)}, s32[8]{0:T(128)}, u32[]{:S(2)}) copy-start(s32[8]{0:T(128)} %get-tuple-element.114) | copy-start | bytes 100 | tf_op jit(solution)/shard_map/while
  78.8 6.4 %copy-start.3 = (s32[8]{0:T(128)S(1)}, s32[8]{0:T(128)}, u32[]{:S(2)}) copy-start(s32[8]{0:T(128)} %get-tuple-element.114) | copy-start | bytes 100 | tf_op jit(solution)/shard_map/while
  88.8 6.4 %copy-start.3 = (s32[8]{0:T(128)S(1)}, s32[8]{0:T(128)}, u32[]{:S(2)}) copy-start(s32[8]{0:T(128)} %get-tuple-element.114) | copy-start | bytes 100 | tf_op jit(solution)/shard_map/while
  98.7 6.4 %copy-start.3 = (s32[8]{0:T(128)S(1)}, s32[8]{0:T(128)}, u32[]{:S(2)}) copy-start(s32[8]{0:T(128)} %get-tuple-element.114) | copy-start | bytes 100 | tf_op jit(solution)/shard_map/while
  108.6 6.4 %copy-start.3 = (s32[8]{0:T(128)S(1)}, s32[8]{0:T(128)}, u32[]{:S(2)}) copy-start(s32[8]{0:T(128)} %get-tuple-element.114) | copy-start | bytes 100 | tf_op jit(solution)/shard_map/while
  118.6 6.4 %copy-start.3 = (s32[8]{0:T(128)S(1)}, s32[8]{0:T(128)}, u32[]{:S(2)}) copy-start(s32[8]{0:T(128)} %get-tuple-element.114) | copy-start | bytes 100 | tf_op jit(solution)/shard_map/while
  128.4 6.4 %copy-start.3 = (s32[8]{0:T(128)S(1)}, s32[8]{0:T(128)}, u32[]{:S(2)}) copy-start(s32[8]{0:T(128)} %get-tuple-element.114) | copy-start | bytes 100 | tf_op jit(solution)/shard_map/while
  137.6 116.9 %copy-start.1 = (f32[128]{0:T(128)S(1)}, f32[128]{0:T(128)}, u32[]{:S(2)}) copy-start(f32[128]{0:T(128)} %param.12) | copy-start | bytes 1540
  137.7 291.7 %reduce-scatter.5.cloned.1.call-start = ((), (), s32[]{:S(2)}) async-start(), calls=%async_computation.4 | async-start | bytes 10616832 | tf_op jit(solution)/shard_map/reduce_scatter | solution.py:47
  265.9 163.5 %copy-start.4 = (u32[32]{0:T(128)S(1)}, u32[32]{0:T(128)}, u32[]{:S(2)}) copy-start(u32[32]{0:T(128)} %constant.33) | copy-start | bytes 388
  265.9 164.8 %copy-start = (f32[128,1536]{1,0:T(8,128)S(1)}, f32[128,1536]{1,0:T(8,128)}, u32[]{:S(2)}) copy-start(f32[128,1536]{1,0:T(8,128)} %reduce-scatter.3.cloned.1.call-done) | copy-start | bytes 2359300
  265.9 164.8 %copy-start.2 = (f32[128]{0:T(128)S(1)}, f32[128]{0:T(128)}, u32[]{:S(2)}) copy-start(f32[128]{0:T(128)} %param.13) | copy-start | bytes 1540
  265.9 202.0 %all-reduce.3.cloned.1.call-start = ((), (), s32[]{:S(2)}) async-start(), calls=%async_computation.5 | async-start | bytes 2359296 | tf_op jit(solution)/shard_map/psum | solution.py:50
Sparse Core Ops, SparseCore 0:
  9.6 48.7 all-gather.1
  137.8 116.7 reduce-scatter.2
  266.0 163.2 reduce-scatter.4
  431.6 36.2 all-reduce.2
where the time goes:
time: 479 us; the launch traced here: 477 us
  waiting for transfers between devices  342 us (71%)
  local copies, waits for them, and re-layouts  56.1 us (12%)
  blocking collectives  25.8 us (5%)
  matrix products  24.6 us (5%)
  between operations  14.5 us (3%)
  other arithmetic  13.3 us (3%)
    reduce_scatter x1, waiting for transfers between devices, on_device(): lax.psum_scatter(gram_term, 'cells', scatter_dimension=0, tiled=True)  163 us
    reduce_scatter x1, waiting for transfers between devices, on_device(): lax.psum_scatter(terms.reshape(lax.axis_size('cells') * own_rows, block_w...  117 us
    all_gather x1, waiting for transfers between devices, on_device(): basis = lax.all_gather(eigen_basis, 'dp', axis=1, tiled=True)  50.4 us
    gather x8, local copies, waits for them, and re-layouts, block_term(): stacked_blocks[column_range].reshape(slot_count * block_tile, block_width)  28.3 us
    dynamic_slice x24, local copies, waits for them, and re-layouts, on_device(): lax.map(lambda items: block_term(items[0], items[1], items[2]), (jac_bloc...  27 us
    unnamed x1, blocking collectives  16.1 us
    dot_general x8, matrix products, block_term(): jnp.dot(masked_entries, selected_rows, preferred_element_type=jnp.float32)  12.7 us
    dot_general x1, matrix products, on_device(): lax.dot_general(jq, weighted, (((0,), (0,)), ((), ())), precision=lax.Pre...  11.3 us
  transfers between devices with their start and end apart: 4, of which 4 were waited for; matrix products, arithmetic and copies ran while one was open for 0% of the time, Pallas kernels for 0%

commit v1 on v0

v1 whole, which is shorter than its diff:
```python
import functools
import math

import jax
import jax.numpy as jnp
from jax import lax
from jax.experimental import pallas as pl
from jax.experimental.pallas import tpu as pltpu
from jax.sharding import PartitionSpec as P

PIECES = 4


def fused(
    n_cells, ndata,
    slots, live, jac, basis, wcol, rcol,
    jq, system, rhs,
    g1, g2, g3, sel, xsend, xrecv, zrecv, u, v, gram, gxr, gzr, vx, vxr, vzr, sysb,
    b_s, b_r, x_s, x_r, z_s, z_r, u_s, u_r, v_s, v_r,
    gx_s, gx_r, gz_s, gz_r, vx_s, vx_r, vz_s, vz_r, s_s, s_r,
):
    f32 = jnp.float32
    half = n_cells // 2
    tile = jac.shape[1]
    slot_count = jac.shape[2] // tile
    width = basis.shape[2]
    depth = basis.shape[0]
    own_rows = gxr.shape[1]
    me, cell = lax.axis_index("dp"), lax.axis_index("cells")
    core, y = me % 2, me // 2
    core_peer = y * 2 + 1 - core
    y_peer = (1 - y) * 2 + core
    far_peer = (1 - y) * 2 + 1 - core
    sources = (me, core_peer, y_peer, far_peer)
    x, line = cell % 2, cell // 2
    x_cell = line * 2 + 1 - x

    def remote(src, dst, send, recv, dp, to_cell):
        return pltpu.make_async_remote_copy(
            src_ref=src, dst_ref=dst, send_sem=send, recv_sem=recv,
            device_id=(dp, to_cell), device_id_type=pl.DeviceIdType.MESH,
        )

    def lanes(source):
        return pl.ds(pl.multiple_of(source * width, 128), width)

    barrier = pltpu.get_barrier_semaphore()
    for dp, to_cell in ((core_peer, cell), (y_peer, cell), (me, x_cell)):
        pl.semaphore_signal(
            barrier, inc=1, device_id=(dp, to_cell), device_id_type=pl.DeviceIdType.MESH
        )

    @pl.loop(1, half)
    def _(k):
        pl.semaphore_signal(
            barrier, inc=1, device_id=(me, (line + k) % half * 2 + x),
            device_id_type=pl.DeviceIdType.MESH,
        )

    pl.semaphore_wait(barrier, 3 + half - 1)

    step = depth // PIECES

    def y_piece(p):
        rows = pl.ds(p * step, step)
        return remote(basis.at[rows], g2.at[rows], b_s.at[1 + p], b_r.at[1 + p], y_peer, cell)

    def on_piece(p):
        rows = pl.ds(p * step, step)
        return remote(
            g2.at[rows], g3.at[rows], b_s.at[1 + PIECES + p], b_r.at[1 + PIECES + p],
            core_peer, cell,
        )

    to_core = remote(basis, g1, b_s.at[0], b_r.at[0], core_peer, cell)
    for p in range(PIECES):
        y_piece(p).start()
    to_core.start()

    chunks = (basis, g1, g2, g3)

    def block_dot(r, b):
        for t in range(slot_count):
            rows = chunks[r][slots[b, t]]
            sel[t * tile:(t + 1) * tile, :] = rows * live[b, t].astype(rows.dtype)
        return jnp.dot(jac[b], sel[...], preferred_element_type=f32)

    def x_copy(r, j):
        return remote(
            xsend.at[r % 2, j], xrecv.at[r, j], x_s.at[r, j], x_r.at[r, j], me, x_cell
        )

    def z_copy(r, j):
        return remote(
            xrecv.at[r, j], zrecv.at[r, line], z_s.at[r, j], z_r.at[r, line], me, 2 * j + x
        )

    def send_x(r):
        @pl.loop(0, half)
        def _(j):
            value = block_dot(r, 2 * j + 1 - x)
            if r >= 2:
                x_copy(r - 2, j).wait_send()
            xsend[r % 2, j] = value
            x_copy(r, j).start()

    def send_z(r):
        @pl.loop(1, half + 1)
        def _(k):
            j = (line + k) % half
            value = block_dot(r, 2 * j + x)
            x_copy(r, j).wait_recv()
            xrecv[r, j] = xrecv[r, j] + value

            @pl.when(k < half)
            def _():
                z_copy(r, j).start()

    def pass_on(p):
        y_piece(p).wait_recv()
        on_piece(p).start()

    send_x(0)
    to_core.wait_recv()
    send_x(1)
    pass_on(0)
    pass_on(1)
    send_z(0)
    pass_on(2)
    pass_on(3)
    send_x(2)
    send_z(1)
    for p in range(PIECES):
        on_piece(p).wait_recv()
    send_x(3)
    send_z(2)
    send_z(3)

    def u_copy(r, to):
        at = u.at[:, 0:tile, lanes(sources[r])]
        dst = u.at[:, (1 + to) * tile:(2 + to) * tile, lanes(sources[r])]
        return remote(at, dst, u_s.at[to, r], u_r.at[to, r], (core_peer, y_peer)[to], cell)

    def u_on(r):
        source = (y_peer, far_peer, me, core_peer)[r]
        return remote(
            u.at[:, 2 * tile:3 * tile, lanes(source)], u.at[:, 3 * tile:4 * tile, lanes(source)],
            u_s.at[2, r], u_r.at[2, r], core_peer, cell,
        )

    for r in range(4):
        @pl.loop(1, half)
        def _(k):
            j = (line + k) % half
            remote(
                xrecv.at[r, j], zrecv.at[r, j], z_s.at[r, j], z_r.at[r, j], me, 2 * j + x
            ).wait_recv()
            xrecv[r, line] = xrecv[r, line] + zrecv[r, j]

        total = xrecv[r, line]
        jq[:, lanes(sources[r])] = total
        scaled = total * wcol[...]
        high = scaled.astype(jnp.bfloat16)
        u[0, 0:tile, lanes(sources[r])] = high
        u[1, 0:tile, lanes(sources[r])] = (scaled - high.astype(f32)).astype(jnp.bfloat16)
        v[0, :, lanes(sources[r])] = jnp.sum(
            (total * rcol[...]).reshape(tile // 8, 8, width), axis=0
        )
        u_copy(r, 1).start()
        u_copy(r, 0).start()

    v_core = remote(v.at[0], v.at[1], v_s.at[0], v_r.at[0], core_peer, cell)
    v_y = remote(v.at[0], v.at[2], v_s.at[1], v_r.at[1], y_peer, cell)
    v_on = remote(v.at[2], v.at[3], v_s.at[2], v_r.at[2], core_peer, cell)
    v_y.start()
    v_core.start()
    for r in range(4):
        u_copy(r, 1).wait_recv()
        u_on(r).start()
    v_y.wait_recv()
    v_on.start()
    for r in range(4):
        u_copy(r, 0).wait_recv()
        u_on(r).wait_recv()
    v_core.wait_recv()
    v_on.wait_recv()

    vx_copy = remote(vx.at[0], vxr, vx_s, vx_r, me, x_cell)
    vx[0] = v[0] + v[1] + v[2] + v[3]
    vx_copy.start()

    m_tile = 256

    @pl.loop(0, gram.shape[0] // m_tile)
    def _(m):
        at = pl.ds(pl.multiple_of(m * m_tile, m_tile), m_tile)

        def product(a, b):
            return lax.dot_general(
                u[a, :, at], u[b, :, lanes(me)], (((0,), (0,)), ((), ())),
                preferred_element_type=f32,
            )

        gram[at, :] = (product(0, 0) + (product(0, 1) + product(1, 0))) / ndata

    def rows_of(c):
        return pl.ds(pl.multiple_of(c * own_rows, 8), own_rows)

    def gx_copy(j):
        return remote(
            gram.at[rows_of(2 * j + 1 - x)], gxr.at[j], gx_s.at[j], gx_r.at[j], me, x_cell
        )

    def gz_copy(j):
        return remote(gxr.at[j], gzr.at[line], gz_s.at[j], gz_r.at[line], me, 2 * j + x)

    def vz_copy(j):
        return remote(vx.at[1], vzr.at[line], vz_s.at[j], vz_r.at[line], me, 2 * j + x)

    @pl.loop(1, half + 1)
    def _(k):
        gx_copy((line + k) % half).start()

    vx_copy.wait_recv()
    vx[1] = vx[0] + vxr[...]

    @pl.loop(1, half)
    def _(k):
        vz_copy((line + k) % half).start()

    @pl.loop(1, half + 1)
    def _(k):
        j = (line + k) % half
        gx_copy(j).wait_recv()
        gxr[j] = gxr[j] + gram[rows_of(2 * j + x), :]

        @pl.when(k < half)
        def _():
            gz_copy(j).start()

    vx[2] = vx[1]
    sysb[0] = gxr[line]

    @pl.loop(1, half)
    def _(k):
        j = (line + k) % half
        remote(
            vx.at[1], vzr.at[j], vz_s.at[j], vz_r.at[j], me, 2 * j + x
        ).wait_recv()
        vx[2] = vx[2] + vzr[j]
        remote(
            gxr.at[j], gzr.at[j], gz_s.at[j], gz_r.at[j], me, 2 * j + x
        ).wait_recv()
        sysb[0] = sysb[0] + gzr[j]

    s_y = remote(sysb.at[0], sysb.at[2], s_s.at[1], s_r.at[1], y_peer, cell)
    s_core = remote(sysb.at[0], sysb.at[1], s_s.at[0], s_r.at[0], core_peer, cell)
    s_on = remote(sysb.at[2], sysb.at[3], s_s.at[2], s_r.at[2], core_peer, cell)
    s_y.start()
    s_core.start()
    rhs[...] = jnp.sum(vx[2], axis=0, keepdims=True) / math.sqrt(ndata)

    def finish(r):
        shape = (own_rows, width)
        row = lax.broadcasted_iota(jnp.int32, shape, 0) + cell * own_rows
        column = lax.broadcasted_iota(jnp.int32, shape, 1) + sources[r] * width
        system[:, lanes(sources[r])] = sysb[r] + (row == column).astype(f32)

    finish(0)
    s_core.wait_recv()
    finish(1)
    s_y.wait_recv()
    s_on.start()
    finish(2)
    s_on.wait_recv()
    finish(3)

    to_core.wait_send()
    for p in range(PIECES):
        y_piece(p).wait_send()
        on_piece(p).wait_send()
    for r in range(4):
        u_copy(r, 0).wait_send()
        u_copy(r, 1).wait_send()
        u_on(r).wait_send()
    for copy in (v_core, v_y, v_on, vx_copy, s_y, s_core, s_on):
        copy.wait_send()

    @pl.loop(1, half + 1)
    def _(k):
        j = (line + k) % half
        x_copy(2, j).wait_send()
        x_copy(3, j).wait_send()
        gx_copy(j).wait_send()

        @pl.when(k < half)
        def _():
            for r in range(4):
                z_copy(r, j).wait_send()
            gz_copy(j).wait_send()
            vz_copy(j).wait_send()


def on_device(jac_blocks, slot_cell_blocks, live_counts, eigen_basis, weights, residual):
    n_cells = lax.axis_size("cells")
    n_groups = lax.axis_size("dp")
    half = n_cells // 2
    tile = jac_blocks.shape[1]
    depth, width = eigen_basis.shape
    full = width * n_groups
    rows_here = full // n_cells
    ndata = weights.shape[0] * n_cells * n_groups
    assert n_groups == 4 and n_cells % 2 == 0
    assert jac_blocks.shape[0] == n_cells and weights.shape[0] == tile
    is_live = (lax.iota(jnp.int32, slot_cell_blocks.shape[1]) < live_counts).astype(jnp.float32)
    wcol = jnp.sqrt(weights)[:, None]
    rcol = (weights * residual)[:, None]
    f32, bf16 = jnp.float32, jnp.bfloat16
    vmem, smem = (pl.BlockSpec(memory_space=s) for s in (pltpu.VMEM, pltpu.SMEM))

    def sems(*shape):
        return [pltpu.SemaphoreType.DMA(shape)] * 2

    jq, system, rhs = pl.pallas_call(
        functools.partial(fused, n_cells, ndata),
        out_shape=(
            jax.ShapeDtypeStruct((tile, full), f32),
            jax.ShapeDtypeStruct((rows_here, full), f32),
            jax.ShapeDtypeStruct((1, full), f32),
        ),
        in_specs=[smem, smem, vmem, vmem, vmem, vmem],
        out_specs=(vmem, vmem, vmem),
        scratch_shapes=[
            pltpu.VMEM((depth // tile, tile, width), bf16),
            pltpu.VMEM((depth // tile, tile, width), bf16),
            pltpu.VMEM((depth // tile, tile, width), bf16),
            pltpu.VMEM((jac_blocks.shape[2], width), bf16),
            pltpu.VMEM((2, half, tile, width), f32),
            pltpu.VMEM((4, half, tile, width), f32),
            pltpu.VMEM((4, half, tile, width), f32),
            pltpu.VMEM((2, 4 * tile, full), bf16),
            pltpu.VMEM((4, 8, full), f32),
            pltpu.VMEM((full, width), f32),
            pltpu.VMEM((half, rows_here, width), f32),
            pltpu.VMEM((half, rows_here, width), f32),
            pltpu.VMEM((3, 8, full), f32),
            pltpu.VMEM((8, full), f32),
            pltpu.VMEM((half, 8, full), f32),
            pltpu.VMEM((4, rows_here, width), f32),
            *sems(1 + 2 * PIECES), *sems(4, half), *sems(4, half), *sems(3, 4), *sems(3),
            *sems(half), *sems(half), *sems(), *sems(half), *sems(3),
        ],
        compiler_params=pltpu.CompilerParams(
            collective_id=0, has_side_effects=True, vmem_limit_bytes=60 * 1024 * 1024
        ),
    )(
        slot_cell_blocks, is_live, jac_blocks,
        eigen_basis.reshape(depth // tile, tile, width), wcol, rcol,
    )
    start = lax.axis_index("cells") * rows_here
    return jq, system, lax.dynamic_slice(rhs[0], (start,), (rows_here,))


def solution(mesh):
    placed = (
        P("dp", None, "cells"),
        P("dp", "cells"),
        P("dp", "cells"),
        P("cells", "dp"),
        P(("dp", "cells")),
        P(("dp", "cells")),
    )
    return jax.shard_map(
        on_device,
        mesh=mesh,
        in_specs=placed,
        out_specs=(P(("dp", "cells"), None), P("cells", None), P("cells")),
        check_vma=False,
    )
```

time: 479 us -> 163 us (0.34)
  waiting for transfers between devices: 342 us -> 0 us
  Pallas kernels: 0 us -> 155 us
  local copies, waits for them, and re-layouts: 56.1 us -> 5.97 us
  blocking collectives: 25.8 us -> 0 us
  matrix products: 24.6 us -> 0 us
  between operations: 14.5 us -> 0.65 us
  other arithmetic: 13.3 us -> 1.99 us
    reduce_scatter x2 -> x0, waiting for transfers between devices: 280 us -> none  [the longest x1 163 us: on_device(): lax.psum_scatter(gram_term, 'cells', scatter_dimension=0, tiled=True)]
    pallas_call x0 -> x1, Pallas kernels: none -> 155 us  [on_device(): pl.pallas_call(functools.partial(fused, n_cells, ndata), out_shape=(jax.S...]
    all_gather x1 -> x0, waiting for transfers between devices: 50.4 us -> none  [on_device(): basis = lax.all_gather(eigen_basis, 'dp', axis=1, tiled=True)]
    gather x8 -> x0, local copies, waits for them, and re-layouts: 28.3 us -> none  [block_term(): stacked_blocks[column_range].reshape(slot_count * block_tile, block_width)]
    dynamic_slice x24 -> x1, local copies, waits for them, and re-layouts: 27 us -> 1.41 us  [on_device(): return (jq, system, lax.dynamic_slice(rhs[0], (start,), (rows_here,)))]
    dot_general x10 -> x0, matrix products: 24.6 us -> none  [the longest x8 12.7 us: block_term(): jnp.dot(masked_entries, selected_rows, preferred_element_type=jnp.float32)]
    unnamed x1 -> x0, blocking collectives: 16.1 us -> none
    psum x1 -> x0, waiting for transfers between devices: 10.8 us -> none  [on_device(): gram_sum, rhs_sum = lax.psum((gram_part, rhs_part), 'dp')]
  transfers between devices with their start and end apart: 4 -> 0, of which waited for: 4 -> 0; matrix products, arithmetic and copies ran while one was open for 0% -> 0% of each run, Pallas kernels for 0% -> 0%
where the time goes in v1:
time: 163 us
  Pallas kernels  155 us (95%)
  local copies, waits for them, and re-layouts  5.97 us (4%)
  other arithmetic  1.99 us (1%)
    pallas_call x1, Pallas kernels, on_device(): pl.pallas_call(functools.partial(fused, n_cells, ndata), out_shape=(jax.S...  155 us

profile of v1, /device:TPU:1, one launch (start us, length us, event | category | flops | bytes accessed | tf_op | source)
XLA Modules:
  0.0 163.2 jit_solution(9795425937142156798)
XLA Ops:
  0.6 0.7 multiply_bitcast_fusion
  1.3 1.3 fusion.live
  2.6 0.7 copy.10.rcol
  3.4 0.7 copy.9.wcol
  4.1 154.6 %shard_map.85 = (f32[128,1536]{1,0:T(8,128)}, f32[192,1536]{1,0:T(8,128)}, f32[1,1536]{1,0:T(1,128)}) custom-call(s32[8,8]{1,0:T(8,128)} %slots.1, f32[8,8]{1,0:T(8,128)} %fusion.live, bf16[8,128,1024]{2,1,0:T(8,128)(2,1)} %jac.1, bf16[16,128,384]{2,1,0:T(8,128)(2,1)} %bitcast.7, f32[128,1]{1,0:T(8,128)} %copy.9.wcol, f32[128,1]{1,0:T(8,128)} %copy.10.rcol), custom_call_target="tpu_custom_call" | custom-call | tf_op jit(solution)/shard_map/pallas_call | solution.py:324
  158.7 0.0 copy-start
  158.8 1.4 constant_dynamic-slice_fusion
  160.2 2.1 %copy.13 = f32[128,1536]{1,0:T(8,128)} copy(f32[128,1536]{1,0:T(8,128)} %get-tuple-element.14) | data formatting | bytes 1572864
  162.2 0.0 copy-done
  162.2 1.0 copy.14
Async XLA Ops:
  158.7 3.5 %copy-start = (f32[192,1536]{1,0:T(8,128)S(1)}, f32[192,1536]{1,0:T(8,128)}, u32[]{:S(2)}) copy-start(f32[192,1536]{1,0:T(8,128)} %get-tuple-element.15) | copy-start | bytes 3538948

commit v2 on v1

v2 whole, which is shorter than its diff:
```python
import functools
import math

import jax
import jax.numpy as jnp
from jax import lax
from jax.experimental import pallas as pl
from jax.experimental.pallas import tpu as pltpu
from jax.sharding import PartitionSpec as P

def code(value):
    top = jnp.maximum(jnp.max(jnp.abs(value), axis=0, keepdims=True), 1e-30)
    whole = jnp.round(value * (32767.0 / top))
    return whole.astype(jnp.int32).astype(jnp.int16), top * (1.0 / 32767.0)


def decode(whole, unit):
    return whole.astype(jnp.int32).astype(jnp.float32) * unit


def fused(
    n_cells, ndata, units,
    slots, live, jac, basis, weights, residual,
    jq, system, rhs,
    g1, g2, g3, sel, xq, xs, xrq, xrs, zrq, zrs, acc, uq, us, u, v,
    gram, gq, gs, gxq, gxs, gzq, gzs, vx, vxr, vzr, sysb,
    b_s, b_r, x_s, x_r, z_s, z_r, u_s, u_r, v_s, v_r,
    gx_s, gx_r, gz_s, gz_r, vx_s, vx_r, vz_s, vz_r, s_s, s_r,
):
    f32 = jnp.float32
    half = n_cells // 2
    tile = jac.shape[1]
    slot_count = jac.shape[2] // tile
    width = basis.shape[2]
    own_rows = gxq.shape[1]
    pieces = width // 128
    me, cell = lax.axis_index("dp"), lax.axis_index("cells")
    core, y = me % 2, me // 2
    core_peer = y * 2 + 1 - core
    y_peer = (1 - y) * 2 + core
    far_peer = (1 - y) * 2 + 1 - core
    sources = (me, core_peer, y_peer, far_peer)
    y_sources = (y_peer, far_peer, me, core_peer)
    x, line = cell % 2, cell // 2
    x_cell = line * 2 + 1 - x

    def remote(src, dst, send, recv, dp, to_cell):
        return pltpu.make_async_remote_copy(
            src_ref=src, dst_ref=dst, send_sem=send, recv_sem=recv,
            device_id=(dp, to_cell), device_id_type=pl.DeviceIdType.MESH,
        )

    def pair(src, dst, send, recv, at, to, dp, to_cell):
        return [
            remote(src[i], dst[i], send.at[(i, *at)], recv.at[(i, *to)], dp, to_cell)
            for i in range(2)
        ]

    def each(verb, copies):
        for copy in copies:
            getattr(copy, verb)()

    def lanes(source, unit=None):
        first, size = (0, width) if unit is None else units[unit][1:]
        return pl.ds(pl.multiple_of(source * width + first, 128), size)

    barrier = pltpu.get_barrier_semaphore()
    for dp, to_cell in ((core_peer, cell), (y_peer, cell), (me, x_cell)):
        pl.semaphore_signal(
            barrier, inc=1, device_id=(dp, to_cell), device_id_type=pl.DeviceIdType.MESH
        )

    @pl.loop(1, half)
    def _(k):
        pl.semaphore_signal(
            barrier, inc=1, device_id=(me, (line + k) % half * 2 + x),
            device_id_type=pl.DeviceIdType.MESH,
        )

    pl.semaphore_wait(barrier, 3 + half - 1)

    def y_piece(p):
        at = (slice(None), slice(None), pl.ds(p * 128, 128))
        return remote(
            basis.at[at], g2[p], b_s.at[1 + p], b_r.at[1 + p], y_peer, cell
        )

    def on_piece(p):
        return remote(
            g2[p], g3[p], b_s.at[1 + pieces + p], b_r.at[1 + pieces + p], core_peer, cell
        )

    to_core = remote(basis, g1, b_s.at[0], b_r.at[0], core_peer, cell)
    for p in range(pieces):
        y_piece(p).start()
    to_core.start()

    def block_dot(n, b):
        r, first, size = units[n]
        held = (basis, g1)[r] if r < 2 else (g2, g3)[r - 2][first // 128]
        for t in range(slot_count):
            rows = held[slots[b, t]]
            keep = jnp.minimum(jnp.maximum(live[b, 0] - t, 0), 1).astype(f32)
            sel[t * tile:(t + 1) * tile, 0:size] = rows * keep.astype(rows.dtype)
        return jnp.dot(jac[b], sel[:, 0:size], preferred_element_type=f32)

    def part(refs, n, j):
        r, first, size = units[n]
        return [ref.at[r, j, :, first:first + size] for ref in refs]

    def x_copy(n, j):
        return pair(
            part((xq, xs), n, j), part((xrq, xrs), n, j), x_s, x_r, (n, j), (n, j), me, x_cell
        )

    def z_copy(n, j, slot):
        return pair(
            part((xrq, xrs), n, j), part((zrq, zrs), n, slot),
            z_s, z_r, (n, j), (n, slot), me, 2 * j + x,
        )

    def send_x(n):
        r, first, size = units[n]

        @pl.loop(0, half)
        def _(j):
            value, unit = code(block_dot(n, 2 * j + 1 - x))
            xq[r, j, :, first:first + size] = value
            xs[r, j, :, first:first + size] = unit
            each("start", x_copy(n, j))

    def send_z(n):
        r, first, size = units[n]
        cols = slice(first, first + size)

        def total(j):
            value = block_dot(n, 2 * j + x)
            each("wait_recv", x_copy(n, j))
            return value + decode(xrq[r, j, :, cols], xrs[r, j, :, cols])

        @pl.loop(1, half)
        def _(k):
            j = (line + k) % half
            value, unit = code(total(j))
            xrq[r, j, :, cols] = value
            xrs[r, j, :, cols] = unit
            each("start", z_copy(n, j, line))

        acc[r, :, cols] = total(line)

    def pass_on(p):
        y_piece(p).wait_recv()
        on_piece(p).start()

    square = (tile, tile)
    wcol = jnp.transpose(jnp.broadcast_to(jnp.sqrt(weights[...]), square))[:, 0:1]
    rcol = jnp.transpose(jnp.broadcast_to(weights[...] * residual[...], square))[:, 0:1]

    def u_part(slot, cols):
        return [uq.at[slot, :, cols], us.at[slot, :, cols]]

    def u_copy(n, to):
        cols = lanes(sources[units[n][0]], n)
        return pair(
            u_part(0, cols), u_part(1 + to, cols), u_s, u_r, (to, n), (to, n),
            (core_peer, y_peer)[to], cell,
        )

    def u_on(n):
        cols = lanes(y_sources[units[n][0]], n)
        return pair(
            u_part(2, cols), u_part(3, cols), u_s, u_r, (2, n), (2, n), core_peer, cell
        )

    def keep_halves(slot, cols, value):
        high = value.astype(jnp.bfloat16)
        at = slice(slot * tile, (slot + 1) * tile)
        u[0, at, cols] = high
        u[1, at, cols] = (value - high.astype(f32)).astype(jnp.bfloat16)

    def finish_rows(n):
        r, first, size = units[n]
        cols = slice(first, first + size)

        @pl.loop(1, half)
        def _(k):
            j = (line + k) % half
            each("wait_recv", z_copy(n, j, j))
            acc[r, :, cols] = acc[r, :, cols] + decode(
                zrq[r, j, :, cols], zrs[r, j, :, cols]
            )

        total = acc[r, :, cols]
        out = lanes(sources[r], n)
        jq[:, out] = total
        scaled = total * wcol
        value, unit = code(scaled)
        uq[0, :, out] = value
        us[0, :, out] = unit
        each("start", u_copy(n, 1))
        each("start", u_copy(n, 0))
        keep_halves(0, out, scaled)
        v[0, :, out] = jnp.sum((total * rcol).reshape(tile // 8, 8, size), axis=0)

    def pass_rows_on(n):
        each("wait_recv", u_copy(n, 1))
        each("start", u_on(n))

    send_x(0)
    to_core.wait_recv()
    send_x(1)
    for p in range(pieces):
        pass_on(p)
        send_x(2 + 2 * p)
        send_z(2 * p)
        if p == pieces - 1:
            finish_rows(0)
        on_piece(p).wait_recv()
        send_x(3 + 2 * p)
        send_z(2 * p + 1)
    finish_rows(1)
    send_z(2 * pieces)
    send_z(2 * pieces + 1)
    pass_rows_on(0)
    pass_rows_on(1)
    for n in range(2, 2 + 2 * pieces):
        finish_rows(n)

    v_core = remote(v.at[0], v.at[1], v_s.at[0], v_r.at[0], core_peer, cell)
    v_y = remote(v.at[0], v.at[2], v_s.at[1], v_r.at[1], y_peer, cell)
    v_on = remote(v.at[2], v.at[3], v_s.at[2], v_r.at[2], core_peer, cell)
    v_y.start()
    v_core.start()

    def take(slot, source, n):
        cols = lanes(source, n)
        keep_halves(slot, cols, decode(uq[slot, :, cols], us[slot, :, cols]))

    for n in range(len(units)):
        r = units[n][0]
        if n >= 2:
            pass_rows_on(n)
        each("wait_recv", u_copy(n, 0))
        take(1, (core_peer, me, far_peer, y_peer)[r], n)
        take(2, y_sources[r], n)
    v_y.wait_recv()
    v_on.start()
    for n in range(len(units)):
        each("wait_recv", u_on(n))
        take(3, (far_peer, y_peer, core_peer, me)[units[n][0]], n)
    v_core.wait_recv()
    v_on.wait_recv()

    vx_copy = remote(vx.at[0], vxr, vx_s, vx_r, me, x_cell)
    vx[0] = v[0] + v[1] + v[2] + v[3]
    vx_copy.start()

    m_tile = 256

    @pl.loop(0, gram.shape[0] // m_tile)
    def _(m):
        at = pl.ds(pl.multiple_of(m * m_tile, m_tile), m_tile)

        def product(a, b):
            return lax.dot_general(
                u[a, :, at], u[b, :, lanes(me)], (((0,), (0,)), ((), ())),
                preferred_element_type=f32,
            )

        gram[at, :] = (product(0, 0) + (product(0, 1) + product(1, 0))) / ndata

    def rows_of(c):
        return pl.ds(pl.multiple_of(c * own_rows, 8), own_rows)

    def gx_copy(j):
        return pair(
            (gq.at[j], gs.at[j]), (gxq.at[j], gxs.at[j]), gx_s, gx_r, (j,), (j,), me, x_cell
        )

    def gz_copy(j, slot):
        return pair(
            (gxq.at[j], gxs.at[j]), (gzq.at[slot], gzs.at[slot]), gz_s, gz_r, (j,), (slot,),
            me, 2 * j + x,
        )

    def vz_copy(j, slot):
        return remote(vx.at[1], vzr.at[slot], vz_s.at[j], vz_r.at[slot], me, 2 * j + x)

    @pl.loop(1, half + 1)
    def _(k):
        j = (line + k) % half
        gq[j], gs[j] = code(gram[rows_of(2 * j + 1 - x), :])
        each("start", gx_copy(j))

    vx_copy.wait_recv()
    vx[1] = vx[0] + vxr[...]

    @pl.loop(1, half)
    def _(k):
        vz_copy((line + k) % half, line).start()

    @pl.loop(1, half)
    def _(k):
        j = (line + k) % half
        each("wait_recv", gx_copy(j))
        gxq[j], gxs[j] = code(decode(gxq[j], gxs[j]) + gram[rows_of(2 * j + x), :])
        each("start", gz_copy(j, line))

    each("wait_recv", gx_copy(line))
    sysb[0] = decode(gxq[line], gxs[line]) + gram[rows_of(cell), :]
    vx[2] = vx[1]

    @pl.loop(1, half)
    def _(k):
        j = (line + k) % half
        vz_copy(j, j).wait_recv()
        vx[2] = vx[2] + vzr[j]
        each("wait_recv", gz_copy(j, j))
        sysb[0] = sysb[0] + decode(gzq[j], gzs[j])

    s_y = remote(sysb.at[0], sysb.at[2], s_s.at[1], s_r.at[1], y_peer, cell)
    s_core = remote(sysb.at[0], sysb.at[1], s_s.at[0], s_r.at[0], core_peer, cell)
    s_on = remote(sysb.at[2], sysb.at[3], s_s.at[2], s_r.at[2], core_peer, cell)
    s_y.start()
    s_core.start()
    rhs[...] = jnp.sum(vx[2], axis=0, keepdims=True) / math.sqrt(ndata)

    def finish(r):
        shape = (own_rows, width)
        row = lax.broadcasted_iota(jnp.int32, shape, 0) + cell * own_rows
        column = lax.broadcasted_iota(jnp.int32, shape, 1) + sources[r] * width
        system[:, lanes(sources[r])] = sysb[r] + (row == column).astype(f32)

    finish(0)
    s_core.wait_recv()
    finish(1)
    s_y.wait_recv()
    s_on.start()
    finish(2)
    s_on.wait_recv()
    finish(3)

    to_core.wait_send()
    for p in range(pieces):
        y_piece(p).wait_send()
        on_piece(p).wait_send()
    for n in range(len(units)):
        each("wait_send", u_copy(n, 0) + u_copy(n, 1) + u_on(n))
    each("wait_send", (v_core, v_y, v_on, vx_copy, s_y, s_core, s_on))

    @pl.loop(1, half + 1)
    def _(k):
        j = (line + k) % half
        for n in range(len(units)):
            each("wait_send", x_copy(n, j))
        each("wait_send", gx_copy(j))

    @pl.loop(1, half)
    def _(k):
        j = (line + k) % half
        for n in range(len(units)):
            each("wait_send", z_copy(n, j, line))
        each("wait_send", gz_copy(j, line))
        vz_copy(j, line).wait_send()


def on_device(jac_blocks, slot_cell_blocks, live_counts, eigen_basis, weights, residual):
    n_cells = lax.axis_size("cells")
    n_groups = lax.axis_size("dp")
    half = n_cells // 2
    tile = jac_blocks.shape[1]
    depth, width = eigen_basis.shape
    full = width * n_groups
    rows_here = full // n_cells
    ndata = weights.shape[0] * n_cells * n_groups
    assert n_groups == 4 and n_cells % 2 == 0 and width % 128 == 0
    assert jac_blocks.shape[0] == n_cells and weights.shape[0] == tile
    units = [(0, 0, width), (1, 0, width)]
    for p in range(width // 128):
        units += [(2, p * 128, 128), (3, p * 128, 128)]
    f32, bf16, i16 = jnp.float32, jnp.bfloat16, jnp.int16
    vmem, smem = (pl.BlockSpec(memory_space=s) for s in (pltpu.VMEM, pltpu.SMEM))

    def sems(*shape):
        return [pltpu.SemaphoreType.DMA(shape)] * 2

    def coded(*lead, rows, columns):
        return [pltpu.VMEM((*lead, rows, columns), i16), pltpu.VMEM((*lead, 1, columns), f32)]

    chunk = pltpu.VMEM((depth // tile, tile, width), bf16)
    piece = pltpu.VMEM((depth // tile, tile, 128), bf16)
    jq, system, rhs = pl.pallas_call(
        functools.partial(fused, n_cells, ndata, tuple(units)),
        out_shape=(
            jax.ShapeDtypeStruct((tile, full), f32),
            jax.ShapeDtypeStruct((rows_here, full), f32),
            jax.ShapeDtypeStruct((1, full), f32),
        ),
        in_specs=[smem, smem, vmem, vmem, vmem, vmem],
        out_specs=(vmem, vmem, vmem),
        scratch_shapes=[
            chunk, (piece,) * (width // 128), (piece,) * (width // 128),
            pltpu.VMEM((jac_blocks.shape[2], width), bf16),
            *coded(4, half, rows=tile, columns=width),
            *coded(4, half, rows=tile, columns=width),
            *coded(4, half, rows=tile, columns=width),
            pltpu.VMEM((4, tile, width), f32),
            *coded(4, rows=tile, columns=full),
            pltpu.VMEM((2, 4 * tile, full), bf16),
            pltpu.VMEM((4, 8, full), f32),
            pltpu.VMEM((full, width), f32),
            *coded(half, rows=rows_here, columns=width),
            *coded(half, rows=rows_here, columns=width),
            *coded(half, rows=rows_here, columns=width),
            pltpu.VMEM((3, 8, full), f32),
            pltpu.VMEM((8, full), f32),
            pltpu.VMEM((half, 8, full), f32),
            pltpu.VMEM((4, rows_here, width), f32),
            *sems(1 + 2 * (width // 128)), *sems(2, len(units), half), *sems(2, len(units), half),
            *sems(2, 3, len(units)), *sems(3),
            *sems(2, half), *sems(2, half), *sems(), *sems(half), *sems(3),
        ],
        compiler_params=pltpu.CompilerParams(
            collective_id=0, has_side_effects=True, vmem_limit_bytes=60 * 1024 * 1024
        ),
    )(
        slot_cell_blocks, live_counts, jac_blocks,
        eigen_basis.reshape(depth // tile, tile, width), weights[None], residual[None],
    )
    start = lax.axis_index("cells") * rows_here
    return jq, system, lax.dynamic_slice(rhs[0], (start,), (rows_here,))


def solution(mesh):
    placed = (
        P("dp", None, "cells"),
        P("dp", "cells"),
        P("dp", "cells"),
        P("cells", "dp"),
        P(("dp", "cells")),
        P(("dp", "cells")),
    )
    return jax.shard_map(
        on_device,
        mesh=mesh,
        in_specs=placed,
        out_specs=(P(("dp", "cells"), None), P("cells", None), P("cells")),
        check_vma=False,
    )
```

time: 163 us -> 107 us (0.66)
  Pallas kernels: 155 us -> 101 us
  other arithmetic: 1.99 us -> 0 us
    pallas_call x1, Pallas kernels: 155 us -> 101 us  [on_device(): pl.pallas_call(functools.partial(fused, n_cells, ndata, tuple(units)), ou...]
    unnamed x4 -> x5, local copies, waits for them, and re-layouts: 3.09 us -> 4.41 us
where the time goes in v2:
time: 107 us
  Pallas kernels  101 us (94%)
  local copies, waits for them, and re-layouts  5.78 us (5%)
    pallas_call x1, Pallas kernels, on_device(): pl.pallas_call(functools.partial(fused, n_cells, ndata, tuple(units)), ou...  101 us
    unnamed x5, local copies, waits for them, and re-layouts  4.41 us

profile of v2, /device:TPU:1, one launch (start us, length us, event | category | flops | bytes accessed | tf_op | source)
XLA Modules:
  0.0 107.0 jit_solution(4041141112993376338)
XLA Ops:
  0.6 1.3 %copy.9.live = s32[8,1]{1,0:T(8,128)} copy(s32[8,1]{0,1:T(1,128)} %param.8) | data formatting | bytes 64 | tf_op args[2]
  2.0 100.6 %shard_map.85 = (f32[128,1536]{1,0:T(8,128)}, f32[192,1536]{1,0:T(8,128)}, f32[1,1536]{1,0:T(1,128)}) custom-call(s32[8,8]{1,0:T(8,128)} %slots.1, s32[8,1]{1,0:T(8,128)} %copy.9.live, bf16[8,128,1024]{2,1,0:T(8,128)(2,1)} %jac.1, bf16[16,128,384]{2,1,0:T(8,128)(2,1)} %bitcast.4, f32[1,128]{1,0:T(1,128)} %bitcast.6, f32[1,128]{1,0:T(1,128)} %bitcast.7), custom_call_target="tpu_custom_call" | custom-call | tf_op jit(solution)/shard_map/pallas_call | solution.py:392
  102.6 0.0 copy-start
  102.6 1.4 %constant_dynamic-slice_fusion = f32[1,192]{1,0:T(1,128)} fusion(f32[1,1536]{1,0:T(1,128)} %get-tuple-element.8, s32[]{:T(128)S(6)} %select_n.3), kind=kLoop, calls=%fused_computation | loop fusion | bytes 1540 | tf_op jit(solution)/shard_map/dynamic_slice | solution.py:431
  104.0 2.1 %copy.12 = f32[128,1536]{1,0:T(8,128)} copy(f32[128,1536]{1,0:T(8,128)} %get-tuple-element.12) | data formatting | bytes 1572864
  106.0 0.0 copy-done
  106.0 1.0 copy.13
Async XLA Ops:
  102.6 3.5 %copy-start = (f32[192,1536]{1,0:T(8,128)S(1)}, f32[192,1536]{1,0:T(8,128)}, u32[]{:S(2)}) copy-start(f32[192,1536]{1,0:T(8,128)} %get-tuple-element.13) | copy-start | bytes 3538948

commit v3 on v2

--- a/solution.py
+++ b/solution.py
@@ -22,7 +22,7 @@
     n_cells, ndata, units,
     slots, live, jac, basis, weights, residual,
     jq, system, rhs,
-    g1, g2, g3, sel, xq, xs, xrq, xrs, zrq, zrs, acc, uq, us, u, v,
+    g1, g2, g3, xq, xs, xrq, xrs, zrq, zrs, acc, uq, us, u, v,
     gram, gq, gs, gxq, gxs, gzq, gzs, vx, vxr, vzr, sysb,
     b_s, b_r, x_s, x_r, z_s, z_r, u_s, u_r, v_s, v_r,
     gx_s, gx_r, gz_s, gz_r, vx_s, vx_r, vz_s, vz_r, s_s, s_r,
@@ -60,9 +60,18 @@
         for copy in copies:
             getattr(copy, verb)()
 
-    def lanes(source, unit=None):
-        first, size = (0, width) if unit is None else units[unit][1:]
+    def lanes(source, first=0, size=width):
         return pl.ds(pl.multiple_of(source * width + first, 128), size)
+
+    def runs(n):
+        at = 0
+        for r, first, size in units[n]:
+            yield r, first, size, slice(at, at + size)
+            at += size
+
+    def span(n):
+        sizes = [sum(size for _, _, size in unit) for unit in units]
+        return slice(sum(sizes[:n]), sum(sizes[:n + 1]))
 
     barrier = pltpu.get_barrier_semaphore()
     for dp, to_cell in ((core_peer, cell), (y_peer, cell), (me, x_cell)):
@@ -96,17 +105,27 @@
     to_core.start()
 
     def block_dot(n, b):
-        r, first, size = units[n]
-        held = (basis, g1)[r] if r < 2 else (g2, g3)[r - 2][first // 128]
-        for t in range(slot_count):
-            rows = held[slots[b, t]]
-            keep = jnp.minimum(jnp.maximum(live[b, 0] - t, 0), 1).astype(f32)
-            sel[t * tile:(t + 1) * tile, 0:size] = rows * keep.astype(rows.dtype)
-        return jnp.dot(jac[b], sel[:, 0:size], preferred_element_type=f32)
+        total = None
+        for t in range(0, slot_count, 2):
+            rows = []
+            for i in (t, t + 1):
+                keep = jnp.minimum(jnp.maximum(live[b, 0] - i, 0), 1).astype(f32)
+                cut = [
+                    (basis, g1)[r][slots[b, i]] if r < 2
+                    else (g2, g3)[r - 2][first // 128][slots[b, i]]
+                    for r, first, _ in units[n]
+                ]
+                row = cut[0] if len(cut) == 1 else jnp.concatenate(cut, axis=1)
+                rows.append(row * keep.astype(row.dtype))
+            term = jnp.dot(
+                jac[b, :, t * tile:(t + 2) * tile], jnp.concatenate(rows, axis=0),
+                preferred_element_type=f32,
+            )
+            total = term if total is None else total + term
+        return total
 
     def part(refs, n, j):
-        r, first, size = units[n]
-        return [ref.at[r, j, :, first:first + size] for ref in refs]
+        return [ref.at[j, :, span(n)] for ref in refs]
 
     def x_copy(n, j):
         return pair(
@@ -120,33 +139,32 @@
         )
 
     def send_x(n):
-        r, first, size = units[n]
-
-        @pl.loop(0, half)
-        def _(j):
-            value, unit = code(block_dot(n, 2 * j + 1 - x))
-            xq[r, j, :, first:first + size] = value
-            xs[r, j, :, first:first + size] = unit
-            each("start", x_copy(n, j))
+        cols = span(n)
+        for k in range(1, half + 1) if half <= 4 else (None,):
+            def one(k):
+                j = (line + k) % half
+                xq[j, :, cols], xs[j, :, cols] = code(block_dot(n, 2 * j + 1 - x))
+                each("start", x_copy(n, j))
+
+            one(k) if k is not None else pl.loop(1, half + 1)(one)
 
     def send_z(n):
-        r, first, size = units[n]
-        cols = slice(first, first + size)
+        cols = span(n)
 
         def total(j):
             value = block_dot(n, 2 * j + x)
             each("wait_recv", x_copy(n, j))
-            return value + decode(xrq[r, j, :, cols], xrs[r, j, :, cols])
-
-        @pl.loop(1, half)
-        def _(k):
-            j = (line + k) % half
-            value, unit = code(total(j))
-            xrq[r, j, :, cols] = value
-            xrs[r, j, :, cols] = unit
-            each("start", z_copy(n, j, line))
-
-        acc[r, :, cols] = total(line)
+            return value + decode(xrq[j, :, cols], xrs[j, :, cols])
+
+        for k in range(1, half) if half <= 4 else (None,):
+            def one(k):
+                j = (line + k) % half
+                xrq[j, :, cols], xrs[j, :, cols] = code(total(j))
+                each("start", z_copy(n, j, line))
+
+            one(k) if k is not None else pl.loop(1, half)(one)
+
+        acc[:, cols] = total(line)
 
     def pass_on(p):
         y_piece(p).wait_recv()
@@ -160,14 +178,14 @@
         return [uq.at[slot, :, cols], us.at[slot, :, cols]]
 
     def u_copy(n, to):
-        cols = lanes(sources[units[n][0]], n)
+        cols = span(n)
         return pair(
             u_part(0, cols), u_part(1 + to, cols), u_s, u_r, (to, n), (to, n),
             (core_peer, y_peer)[to], cell,
         )
 
     def u_on(n):
-        cols = lanes(y_sources[units[n][0]], n)
+        cols = span(n)
         return pair(
             u_part(2, cols), u_part(3, cols), u_s, u_r, (2, n), (2, n), core_peer, cell
         )
@@ -179,28 +197,25 @@
         u[1, at, cols] = (value - high.astype(f32)).astype(jnp.bfloat16)
 
     def finish_rows(n):
-        r, first, size = units[n]
-        cols = slice(first, first + size)
+        cols = span(n)
 
         @pl.loop(1, half)
         def _(k):
             j = (line + k) % half
             each("wait_recv", z_copy(n, j, j))
-            acc[r, :, cols] = acc[r, :, cols] + decode(
-                zrq[r, j, :, cols], zrs[r, j, :, cols]
-            )
-
-        total = acc[r, :, cols]
-        out = lanes(sources[r], n)
-        jq[:, out] = total
+            acc[:, cols] = acc[:, cols] + decode(zrq[j, :, cols], zrs[j, :, cols])
+
+        total = acc[:, cols]
         scaled = total * wcol
-        value, unit = code(scaled)
-        uq[0, :, out] = value
-        us[0, :, out] = unit
+        uq[0, :, cols], us[0, :, cols] = code(scaled)
         each("start", u_copy(n, 1))
         each("start", u_copy(n, 0))
-        keep_halves(0, out, scaled)
-        v[0, :, out] = jnp.sum((total * rcol).reshape(tile // 8, 8, size), axis=0)
+        misfit = jnp.sum((total * rcol).reshape(tile // 8, 8, total.shape[1]), axis=0)
+        for r, first, size, at in runs(n):
+            out = lanes(sources[r], first, size)
+            jq[:, out] = total[:, at]
+            v[0, :, out] = misfit[:, at]
+            keep_halves(0, out, scaled[:, at])
 
     def pass_rows_on(n):
         each("wait_recv", u_copy(n, 1))
@@ -211,19 +226,18 @@
     send_x(1)
     for p in range(pieces):
         pass_on(p)
-        send_x(2 + 2 * p)
-        send_z(2 * p)
-        if p == pieces - 1:
-            finish_rows(0)
+        if p < 2:
+            send_z(p)
+        else:
+            send_z(p)
+            finish_rows(p - 2)
         on_piece(p).wait_recv()
-        send_x(3 + 2 * p)
-        send_z(2 * p + 1)
-    finish_rows(1)
-    send_z(2 * pieces)
-    send_z(2 * pieces + 1)
-    pass_rows_on(0)
-    pass_rows_on(1)
-    for n in range(2, 2 + 2 * pieces):
+        send_x(2 + p)
+    send_z(pieces)
+    finish_rows(pieces - 2)
+    send_z(pieces + 1)
+    for n in range(pieces - 1, pieces + 2):
+        pass_rows_on(n - pieces + 1)
         finish_rows(n)
 
     v_core = remote(v.at[0], v.at[1], v_s.at[0], v_r.at[0], core_peer, cell)
@@ -232,22 +246,22 @@
     v_y.start()
     v_core.start()
 
-    def take(slot, source, n):
-        cols = lanes(source, n)
-        keep_halves(slot, cols, decode(uq[slot, :, cols], us[slot, :, cols]))
+    def take(slot, order, n):
+        value = decode(uq[slot, :, span(n)], us[slot, :, span(n)])
+        for r, first, size, at in runs(n):
+            keep_halves(slot, lanes(order[r], first, size), value[:, at])
 
     for n in range(len(units)):
-        r = units[n][0]
-        if n >= 2:
+        if n >= 3:
             pass_rows_on(n)
         each("wait_recv", u_copy(n, 0))
-        take(1, (core_peer, me, far_peer, y_peer)[r], n)
-        take(2, y_sources[r], n)
+        take(1, (core_peer, me, far_peer, y_peer), n)
+        take(2, y_sources, n)
     v_y.wait_recv()
     v_on.start()
     for n in range(len(units)):
         each("wait_recv", u_on(n))
-        take(3, (far_peer, y_peer, core_peer, me)[units[n][0]], n)
+        take(3, (far_peer, y_peer, core_peer, me), n)
     v_core.wait_recv()
     v_on.wait_recv()
 
@@ -375,9 +389,8 @@
     ndata = weights.shape[0] * n_cells * n_groups
     assert n_groups == 4 and n_cells % 2 == 0 and width % 128 == 0
     assert jac_blocks.shape[0] == n_cells and weights.shape[0] == tile
-    units = [(0, 0, width), (1, 0, width)]
-    for p in range(width // 128):
-        units += [(2, p * 128, 128), (3, p * 128, 128)]
+    units = [((0, 0, width),), ((1, 0, width),)]
+    units += [((2, p * 128, 128), (3, p * 128, 128)) for p in range(width // 128)]
     f32, bf16, i16 = jnp.float32, jnp.bfloat16, jnp.int16
     vmem, smem = (pl.BlockSpec(memory_space=s) for s in (pltpu.VMEM, pltpu.SMEM))
 
@@ -400,11 +413,10 @@
         out_specs=(vmem, vmem, vmem),
         scratch_shapes=[
             chunk, (piece,) * (width // 128), (piece,) * (width // 128),
-            pltpu.VMEM((jac_blocks.shape[2], width), bf16),
-            *coded(4, half, rows=tile, columns=width),
-            *coded(4, half, rows=tile, columns=width),
-            *coded(4, half, rows=tile, columns=width),
-            pltpu.VMEM((4, tile, width), f32),
+            *coded(half, rows=tile, columns=full),
+            *coded(half, rows=tile, columns=full),
+            *coded(half, rows=tile, columns=full),
+            pltpu.VMEM((tile, full), f32),
             *coded(4, rows=tile, columns=full),
             pltpu.VMEM((2, 4 * tile, full), bf16),
             pltpu.VMEM((4, 8, full), f32),

time: 107 us -> 110 us (1.028)
  Pallas kernels: 101 us -> 103 us
    pallas_call x1, Pallas kernels: 101 us -> 103 us  [on_device(): pl.pallas_call(functools.partial(fused, n_cells, ndata, tuple(units)), ou...]
where the time goes in v3:
time: 110 us
  Pallas kernels  103 us (94%)
  local copies, waits for them, and re-layouts  5.78 us (5%)
    pallas_call x1, Pallas kernels, on_device(): pl.pallas_call(functools.partial(fused, n_cells, ndata, tuple(units)), ou...  103 us
    unnamed x5, local copies, waits for them, and re-layouts  4.41 us

profile of v3, /device:TPU:1, one launch (start us, length us, event | category | flops | bytes accessed | tf_op | source)
XLA Modules:
  0.0 109.8 jit_solution(11353757416306826593)
XLA Ops:
  0.6 1.3 %copy.9.live = s32[8,1]{1,0:T(8,128)} copy(s32[8,1]{0,1:T(1,128)} %param.8) | data formatting | bytes 64 | tf_op args[2]
  2.0 103.4 %shard_map.85 = (f32[128,1536]{1,0:T(8,128)}, f32[192,1536]{1,0:T(8,128)}, f32[1,1536]{1,0:T(1,128)}) custom-call(s32[8,8]{1,0:T(8,128)} %slots.1, s32[8,1]{1,0:T(8,128)} %copy.9.live, bf16[8,128,1024]{2,1,0:T(8,128)(2,1)} %jac.1, bf16[16,128,384]{2,1,0:T(8,128)(2,1)} %bitcast.4, f32[1,128]{1,0:T(1,128)} %bitcast.6, f32[1,128]{1,0:T(1,128)} %bitcast.7), custom_call_target="tpu_custom_call" | custom-call | tf_op jit(solution)/shard_map/pallas_call | solution.py:405
  105.3 0.0 copy-start
  105.4 1.4 %constant_dynamic-slice_fusion = f32[1,192]{1,0:T(1,128)} fusion(f32[1,1536]{1,0:T(1,128)} %get-tuple-element.8, s32[]{:T(128)S(6)} %select_n.3), kind=kLoop, calls=%fused_computation | loop fusion | bytes 1540 | tf_op jit(solution)/shard_map/dynamic_slice | solution.py:443
  106.7 2.1 %copy.12 = f32[128,1536]{1,0:T(8,128)} copy(f32[128,1536]{1,0:T(8,128)} %get-tuple-element.12) | data formatting | bytes 1572864
  108.8 0.0 copy-done
  108.8 1.0 copy.13
Async XLA Ops:
  105.3 3.5 %copy-start = (f32[192,1536]{1,0:T(8,128)S(1)}, f32[192,1536]{1,0:T(8,128)}, u32[]{:S(2)}) copy-start(f32[192,1536]{1,0:T(8,128)} %get-tuple-element.13) | copy-start | bytes 3538948

commit v4 on v2

--- a/solution.py
+++ b/solution.py
@@ -23,7 +23,7 @@
     slots, live, jac, basis, weights, residual,
     jq, system, rhs,
     g1, g2, g3, sel, xq, xs, xrq, xrs, zrq, zrs, acc, uq, us, u, v,
-    gram, gq, gs, gxq, gxs, gzq, gzs, vx, vxr, vzr, sysb,
+    gram, gq, gs, gxq, gxs, gzq, gzs, vx, vxr, vzr, sysb, sq, su,
     b_s, b_r, x_s, x_r, z_s, z_r, u_s, u_r, v_s, v_r,
     gx_s, gx_r, gz_s, gz_r, vx_s, vx_r, vz_s, vz_r, s_s, s_r,
 ):
@@ -100,7 +100,7 @@
         held = (basis, g1)[r] if r < 2 else (g2, g3)[r - 2][first // 128]
         for t in range(slot_count):
             rows = held[slots[b, t]]
-            keep = jnp.minimum(jnp.maximum(live[b, 0] - t, 0), 1).astype(f32)
+            keep = jnp.minimum(jnp.maximum(live[b] - t, 0), 1).astype(f32)
             sel[t * tile:(t + 1) * tile, 0:size] = rows * keep.astype(rows.dtype)
         return jnp.dot(jac[b], sel[:, 0:size], preferred_element_type=f32)
 
@@ -307,7 +307,7 @@
         each("start", gz_copy(j, line))
 
     each("wait_recv", gx_copy(line))
-    sysb[0] = decode(gxq[line], gxs[line]) + gram[rows_of(cell), :]
+    sysb[...] = decode(gxq[line], gxs[line]) + gram[rows_of(cell), :]
     vx[2] = vx[1]
 
     @pl.loop(1, half)
@@ -316,28 +316,36 @@
         vz_copy(j, j).wait_recv()
         vx[2] = vx[2] + vzr[j]
         each("wait_recv", gz_copy(j, j))
-        sysb[0] = sysb[0] + decode(gzq[j], gzs[j])
-
-    s_y = remote(sysb.at[0], sysb.at[2], s_s.at[1], s_r.at[1], y_peer, cell)
-    s_core = remote(sysb.at[0], sysb.at[1], s_s.at[0], s_r.at[0], core_peer, cell)
-    s_on = remote(sysb.at[2], sysb.at[3], s_s.at[2], s_r.at[2], core_peer, cell)
-    s_y.start()
-    s_core.start()
-    rhs[...] = jnp.sum(vx[2], axis=0, keepdims=True) / math.sqrt(ndata)
+        sysb[...] = sysb[...] + decode(gzq[j], gzs[j])
+
+    def s_copy(i, src, dst, dp):
+        return pair(
+            (sq.at[src], su.at[src]), (sq.at[dst], su.at[dst]), s_s, s_r, (i,), (i,), dp, cell
+        )
+
+    sq[0], su[0] = code(sysb[...])
+    s_y, s_core, s_on = s_copy(1, 0, 2, y_peer), s_copy(0, 0, 1, core_peer), s_copy(2, 2, 3, core_peer)
+    each("start", s_y)
+    each("start", s_core)
+    misfit = jnp.sum(vx[2], axis=0, keepdims=True) / math.sqrt(ndata)
+    own = jnp.zeros(rhs.shape, f32)
+    for c in range(n_cells):
+        own = jnp.where(cell == c, misfit[:, c * own_rows:(c + 1) * own_rows], own)
+    rhs[...] = own
 
     def finish(r):
         shape = (own_rows, width)
         row = lax.broadcasted_iota(jnp.int32, shape, 0) + cell * own_rows
         column = lax.broadcasted_iota(jnp.int32, shape, 1) + sources[r] * width
-        system[:, lanes(sources[r])] = sysb[r] + (row == column).astype(f32)
+        system[:, lanes(sources[r])] = decode(sq[r], su[r]) + (row == column).astype(f32)
 
     finish(0)
-    s_core.wait_recv()
+    each("wait_recv", s_core)
     finish(1)
-    s_y.wait_recv()
-    s_on.start()
+    each("wait_recv", s_y)
+    each("start", s_on)
     finish(2)
-    s_on.wait_recv()
+    each("wait_recv", s_on)
     finish(3)
 
     to_core.wait_send()
@@ -346,7 +354,7 @@
         on_piece(p).wait_send()
     for n in range(len(units)):
         each("wait_send", u_copy(n, 0) + u_copy(n, 1) + u_on(n))
-    each("wait_send", (v_core, v_y, v_on, vx_copy, s_y, s_core, s_on))
+    each("wait_send", [v_core, v_y, v_on, vx_copy] + s_y + s_core + s_on)
 
     @pl.loop(1, half + 1)
     def _(k):
@@ -394,7 +402,7 @@
         out_shape=(
             jax.ShapeDtypeStruct((tile, full), f32),
             jax.ShapeDtypeStruct((rows_here, full), f32),
-            jax.ShapeDtypeStruct((1, full), f32),
+            jax.ShapeDtypeStruct((1, rows_here), f32),
         ),
         in_specs=[smem, smem, vmem, vmem, vmem, vmem],
         out_specs=(vmem, vmem, vmem),
@@ -415,20 +423,20 @@
             pltpu.VMEM((3, 8, full), f32),
             pltpu.VMEM((8, full), f32),
             pltpu.VMEM((half, 8, full), f32),
-            pltpu.VMEM((4, rows_here, width), f32),
+            pltpu.VMEM((rows_here, width), f32),
+            *coded(4, rows=rows_here, columns=width),
             *sems(1 + 2 * (width // 128)), *sems(2, len(units), half), *sems(2, len(units), half),
             *sems(2, 3, len(units)), *sems(3),
-            *sems(2, half), *sems(2, half), *sems(), *sems(half), *sems(3),
+            *sems(2, half), *sems(2, half), *sems(), *sems(half), *sems(2, 3),
         ],
         compiler_params=pltpu.CompilerParams(
             collective_id=0, has_side_effects=True, vmem_limit_bytes=60 * 1024 * 1024
         ),
     )(
-        slot_cell_blocks, live_counts, jac_blocks,
+        slot_cell_blocks, live_counts[:, 0], jac_blocks,
         eigen_basis.reshape(depth // tile, tile, width), weights[None], residual[None],
     )
-    start = lax.axis_index("cells") * rows_here
-    return jq, system, lax.dynamic_slice(rhs[0], (start,), (rows_here,))
+    return jq, system, rhs[0]
 
 
 def solution(mesh):

time: 107 us -> 102 us (0.953)
  Pallas kernels: 101 us -> 97.5 us
  local copies, waits for them, and re-layouts: 5.78 us -> 3.75 us
    pallas_call x1, Pallas kernels: 101 us -> 97.5 us  [on_device(): pl.pallas_call(functools.partial(fused, n_cells, ndata, tuple(units)), ou...]
    dynamic_slice x1 -> x0, local copies, waits for them, and re-layouts: 1.38 us -> none  [on_device(): return (jq, system, lax.dynamic_slice(rhs[0], (start,), (rows_here,)))]
    unnamed x5 -> x7, local copies, waits for them, and re-layouts: 4.41 us -> 3.75 us
where the time goes in v4:
time: 102 us
  Pallas kernels  97.5 us (96%)
  local copies, waits for them, and re-layouts  3.75 us (4%)
    pallas_call x1, Pallas kernels, on_device(): pl.pallas_call(functools.partial(fused, n_cells, ndata, tuple(units)), ou...  97.5 us
    unnamed x7, local copies, waits for them, and re-layouts  3.75 us

profile of v4, /device:TPU:1, one launch (start us, length us, event | category | flops | bytes accessed | tf_op | source)
XLA Modules:
  0.0 101.8 jit_solution(15164674231379487935)
XLA Ops:
  0.6 97.5 %shard_map.85 = (f32[128,1536]{1,0:T(8,128)}, f32[192,1536]{1,0:T(8,128)}, f32[1,192]{1,0:T(1,128)}) custom-call(s32[8,8]{1,0:T(8,128)} %slots.1, s32[8]{0:T(128)} %bitcast.7, bf16[8,128,1024]{2,1,0:T(8,128)(2,1)} %jac.1, bf16[16,128,384]{2,1,0:T(8,128)(2,1)} %bitcast.5, f32[1,128]{1,0:T(1,128)} %bitcast.8, f32[1,128]{1,0:T(1,128)} %bitcast.9), custom_call_target="tpu_custom_call" | custom-call | tf_op jit(solution)/shard_map/pallas_call | solution.py:400
  98.1 0.0 copy-start
  98.1 2.2 %copy.12 = f32[128,1536]{1,0:T(8,128)} copy(f32[128,1536]{1,0:T(8,128)} %get-tuple-element.12) | data formatting | bytes 1572864
  100.3 0.0 copy-done
  100.3 0.0 copy-start.1
  100.3 1.0 copy.13
  101.3 0.0 copy-done.1
  101.3 0.6 copy.14
Async XLA Ops:
  98.1 2.2 %copy-start = (f32[192,1536]{1,0:T(8,128)S(1)}, f32[192,1536]{1,0:T(8,128)}, u32[]{:S(2)}) copy-start(f32[192,1536]{1,0:T(8,128)} %get-tuple-element.13) | copy-start | bytes 3538948
  100.3 1.0 copy-start.1
